TPU v7x, 256 devices: a whole 4x4x8 slice. The times are simulated.
256 devices in a mesh: replica: 4 (over y_lo, core), fsdp: 8 (over z), tensor: 8 (over x, y_hi).
Axes of the slice: x: 4, y: 4 (y_hi: 2, y_lo: 2; y = y_hi * 2 + y_lo), z: 8, core: 2. Of those that a mesh axis runs over, the one named last changes fastest.
Arguments:
- tokens: bfloat16 [16384, 8192], P(('replica', 'fsdp')), may hold values from -6 to 6
- norm_gain: float32 [8192], replicated, may hold values from 0.1 to 1.9
- outer_base: float32 [2, 8192, 1024], P(None, 'fsdp', 'tensor'), may hold values from -0.0625 to 0.0625
- momentum: float32 [2, 8192, 1024], P(None, 'fsdp', 'tensor'), may hold values from -0.06 to 0.06
- inner_params: bfloat16 [4, 2, 8192, 1024], P('replica', None, 'fsdp', 'tensor'), may hold values from -0.0625 to 0.0625
Outputs:
- new_base: float32 [2, 8192, 1024], P(None, ('fsdp', 'replica'), 'tensor')
- new_momentum: float32 [2, 8192, 1024], P(None, ('fsdp', 'replica'), 'tensor')
- keys: bfloat16 [16384, 1024], P(('replica', 'fsdp'), 'tensor')
- values: bfloat16 [16384, 1024], P(('replica', 'fsdp'), 'tensor')
All inputs are finite; a program needn't handle non-finite values.
Results may differ from a plain program's by a relative error of at most 0.018.
Values may be sent and summed in bfloat16 or wider, within the bound.
No kernel may reach another device: no remote copies, remote signals or barrier semaphores. Data moves between devices by JAX's collectives and lax.ppermute only.
A program may use at most 64 MiB of HBM per device.

v0:
```python
import jax
import jax.numpy as jnp
from jax import lax
from jax.sharding import PartitionSpec as P

momentum_rate = 0.9
outer_rate = 0.7
epsilon = 1e-05


def sent_to_all(x, axis):
    copies = jnp.broadcast_to(x, (lax.axis_size(axis), *x.shape))
    return lax.all_to_all(copies, axis, split_axis=0, concat_axis=0, tiled=True)


def taken_together(x, axis):
    everything = sent_to_all(x, axis)
    return jnp.sum(everything.astype(jnp.float32), axis=0)


def normalize(tokens, norm_gain):
    inputs = tokens.astype(jnp.float32)
    scale = lax.rsqrt(jnp.mean(inputs * inputs, axis=-1, keepdims=True) + epsilon)
    return (inputs * scale * norm_gain).astype(jnp.bfloat16)


def nesterov(outer_base, momentum, average):
    new_momentum = momentum_rate * momentum + average
    new_base = outer_base - outer_rate * (average + momentum_rate * new_momentum)
    return (new_base, new_momentum)


def make_adder(normed, portion):
    first = jnp.dot(normed, portion[0], preferred_element_type=jnp.float32)
    second = jnp.dot(normed, portion[1], preferred_element_type=jnp.float32)
    return (first, second)


def on_device(tokens, norm_gain, outer_base, momentum, inner_params):
    normed = normalize(tokens, norm_gain)
    deltas = (outer_base - inner_params[0].astype(jnp.float32)).astype(jnp.bfloat16)
    replicas = lax.axis_size("replica")
    shard_rows = outer_base.shape[1]
    quarter = shard_rows // replicas
    replica_index = lax.axis_index("replica")
    terms = deltas.astype(jnp.float32)
    summed = taken_together(terms.astype(jnp.bfloat16), "replica").astype(jnp.float32)
    full_base, full_momentum = nesterov(outer_base, momentum, summed / replicas)
    weights = full_base.astype(jnp.bfloat16)
    keys, values = make_adder(normed, lax.all_gather(weights, "fsdp", axis=1, tiled=True))
    new_base = lax.dynamic_slice_in_dim(full_base, replica_index * quarter, quarter, 1)
    new_momentum = lax.dynamic_slice_in_dim(full_momentum, replica_index * quarter, quarter, 1)
    return (new_base, new_momentum, keys.astype(jnp.bfloat16), values.astype(jnp.bfloat16))


def solution(mesh):
    placed = (
        P(("replica", "fsdp"), None),
        P(),
        P(None, "fsdp", "tensor"),
        P(None, "fsdp", "tensor"),
        P("replica", None, "fsdp", "tensor"),
    )
    return jax.shard_map(
        on_device,
        mesh=mesh,
        in_specs=placed,
        out_specs=(
            P(None, ("fsdp", "replica"), "tensor"),
            P(None, ("fsdp", "replica"), "tensor"),
            P(("replica", "fsdp"), "tensor"),
            P(("replica", "fsdp"), "tensor"),
        ),
        check_vma=False,
    )
```

profile of v0, /device:TPU:1, one launch (start us, length us, event | category | flops | bytes accessed | tf_op | source)
XLA Modules:
  0.0 117.8 jit_solution(4848803696072113778)
XLA Ops:
  7.2 0.0 copy-start
  7.2 0.0 all-gather.2.cloned.1.call-start
  7.2 0.0 copy-start.1
  7.2 1.6 %fusion.13 = bf16[2,1024,128]{2,1,0:T(8,128)(2,1)S(1)} fusion(f32[2,1024,128]{2,1,0:T(8,128)} %param.7, bf16[1,2,1024,128]{3,2,1,0:T(8,128)(2,1)} %param.9), kind=kLoop, calls=%fused_computation.13 | loop fusion | flops 786432 | bytes 2097152 | tf_op jit(solution)/shard_map/convert_element_type | solution.py:41
  8.8 0.3 broadcast_in_dim.2
  9.1 30.3 %all_to_all.5 = bf16[4,2,1024,128]{3,2,1,0:T(8,128)(2,1)S(1)} all-to-all(bf16[4,2,1024,128]{3,2,1,0:T(8,128)(2,1)S(1)} %broadcast_in_dim.2), channel_id=1, replica_groups=mesh['replica'=4,'fsdp'=8,'tensor'=8] {'replica'}, dimensions={0} | all-to-all | bytes 4194304 | tf_op jit(solution)/shard_map/all_to_all | solution.py:13
  39.4 0.3 convert_reduce_fusion
  39.7 0.0 copy-done
  39.7 0.0 copy-done.1
  39.8 0.0 copy-start.3
  39.8 1.2 fusion.14
  40.9 0.0 all-gather.2.cloned.1.call-update
  41.0 5.1 %fusion = f32[512]{0:T(512)S(1)} fusion(bf16[512,8192]{1,0:T(8,128)(2,1)} %param.5), kind=kLoop, calls=%fused_computation.2 | loop fusion | flops 12582400 | bytes 8390656 | tf_op jit(solution)/shard_map/reduce_sum | solution.py:23
  46.1 0.8 constant_dynamic-slice_fusion
  46.9 50.4 %all-gather.2.cloned.1.call-done = bf16[2,8192,128]{2,1,0:T(8,128)(2,1)} async-done(((bf16[2,1024,128]{2,1,0:T(8,128)(2,1)}), bf16[2,8192,128]{2,1,0:T(8,128)(2,1)}) %all-gather.2.cloned.1.call-update) | async-done | bytes 4194320 | tf_op jit(solution)/shard_map/all_gather | solution.py:50
  97.3 0.0 copy-done.3
  97.3 0.0 copy-start.2
  97.3 7.2 %fusion.10 = bf16[512,128]{1,0:T(8,128)(2,1)} fusion(bf16[2,8192,128]{2,1,0:T(8,128)(2,1)} %all-gather.2.cloned.1.call-done, bf16[512,8192]{1,0:T(8,128)(2,1)} %param.5, f32[8192]{0:T(1024)S(1)} %copy-done.3, f32[512]{0:T(512)S(1)} %add_rsqrt_fusion), kind=kOutput, calls=%fused_computation.11 | convolution fusion | flops 1090584576 | bytes 10651648 | tf_op jit(solution)/shard_map/dot_general | solution.py:35
  104.5 0.0 copy-done.2
  104.5 6.4 %fusion.7 = bf16[512,128]{1,0:T(8,128)(2,1)} fusion(bf16[2,8192,128]{2,1,0:T(8,128)(2,1)S(1)} %copy-done.2, bf16[512,8192]{1,0:T(8,128)(2,1)} %param.5, f32[8192]{0:T(1024)S(1)} %copy-done.3, f32[512]{0:T(512)S(1)} %add_rsqrt_fusion), kind=kOutput, calls=%fused_computation.10 | convolution fusion | flops 1090584576 | bytes 10651648 | tf_op jit(solution)/shard_map/dot_general | solution.py:34
  (1 shorter events, 0.0 us)
Async XLA Ops:
  7.2 32.6 %copy-start = (f32[2,1024,128]{2,1,0:T(8,128)S(1)}, f32[2,1024,128]{2,1,0:T(8,128)}, u32[]{:S(2)}) copy-start(f32[2,1024,128]{2,1,0:T(8,128)} %param.7) | copy-start | bytes 3145732
  7.2 90.2 %all-gather.2.cloned.1.call-start = ((), (), s32[]{:S(2)}) async-start(), calls=%async_computation.1 | async-start | bytes 4718592 | tf_op jit(solution)/shard_map/all_gather | solution.py:50
  7.2 32.5 %copy-start.1 = (f32[2,1024,128]{2,1,0:T(8,128)S(1)}, f32[2,1024,128]{2,1,0:T(8,128)}, u32[]{:S(2)}) copy-start(f32[2,1024,128]{2,1,0:T(8,128)} %param.8) | copy-start | bytes 3145732
  39.8 57.6 %copy-start.3 = (f32[8192]{0:T(1024)S(1)}, f32[8192]{0:T(1024)}, u32[]{:S(2)}) copy-start(f32[8192]{0:T(1024)} %param.6) | copy-start | bytes 98308
  97.3 7.2 %copy-start.2 = (bf16[2,8192,128]{2,1,0:T(8,128)(2,1)S(1)}, bf16[2,8192,128]{2,1,0:T(8,128)(2,1)}, u32[]{:S(2)}) copy-start(bf16[2,8192,128]{2,1,0:T(8,128)(2,1)} %all-gather.2.cloned.1.call-done) | copy-start | bytes 12582916
Sparse Core Ops, SparseCore 0:
  41.1 56.2 all-gather.1
where the time goes:
time: 118 us
  waiting for transfers between devices  50.4 us (43%)
  blocking collectives  30.3 us (26%)
  between operations  14.1 us (12%)
  matrix products  13.6 us (12%)
  other arithmetic  8.2 us (7%)
    all_gather x1, waiting for transfers between devices, on_device(): lax.all_gather(weights, 'fsdp', axis=1, tiled=True)  50.4 us
    all_to_all x1, blocking collectives, sent_to_all(): return lax.all_to_all(copies, axis, split_axis=0, concat_axis=0, tiled=True)  30.3 us
    dot_general x1, matrix products, make_adder(): second = jnp.dot(normed, portion[1], preferred_element_type=jnp.float32)  7.16 us
    dot_general x1, matrix products, make_adder(): first = jnp.dot(normed, portion[0], preferred_element_type=jnp.float32)  6.43 us
    reduce_sum x1, other arithmetic, normalize(): jnp.mean(inputs * inputs, axis=-1, keepdims=True) + epsilon  5.1 us
  transfers between devices with their start and end apart: 1, of which 1 were waited for; matrix products, arithmetic and copies ran while one was open for 5% of the time, Pallas kernels for 0%

commit v1 on v0

--- a/solution.py
+++ b/solution.py
@@ -1,3 +1,4 @@
+import functools
 import jax
 import jax.numpy as jnp
 from jax import lax
@@ -6,6 +7,39 @@
 momentum_rate = 0.9
 outer_rate = 0.7
 epsilon = 1e-05
+
+
+def test_the_local_data(block_in, bus_axis):
+    vec_out, state_now, last = (
+        lax.axis_size(bus_axis),
+        lax.axis_index(bus_axis),
+        block_in.shape[1],
+    )
+    series = tuple(
+        (hop_no * vec_out if b == 1 else hop_no for b, hop_no in enumerate(block_in.shape))
+    )
+    back = lax.dynamic_update_slice_in_dim(
+        jnp.zeros(series, block_in.dtype), block_in, state_now * last, axis=1
+    )
+    met_up = low = block_in
+    for u in range(1, vec_out // 2 + 1):
+        met_up = lax.ppermute(
+            met_up, bus_axis, tuple(((b, (b + 1) % vec_out) for b in range(vec_out)))
+        )
+        back = lax.dynamic_update_slice_in_dim(
+            back, met_up, (state_now - u) % vec_out * last, axis=1
+        )
+        if 2 * u < vec_out:
+            low = lax.ppermute(
+                low, bus_axis, tuple(((b, (b - 1) % vec_out) for b in range(vec_out)))
+            )
+            back = lax.dynamic_update_slice_in_dim(
+                back, low, (state_now + u) % vec_out * last, axis=1
+            )
+    return back
+
+
+raise_sides_all = functools.partial(test_the_local_data, bus_axis="fsdp")
 
 
 def sent_to_all(x, axis):
@@ -47,7 +81,7 @@
     summed = taken_together(terms.astype(jnp.bfloat16), "replica").astype(jnp.float32)
     full_base, full_momentum = nesterov(outer_base, momentum, summed / replicas)
     weights = full_base.astype(jnp.bfloat16)
-    keys, values = make_adder(normed, lax.all_gather(weights, "fsdp", axis=1, tiled=True))
+    keys, values = make_adder(normed, raise_sides_all(weights))
     new_base = lax.dynamic_slice_in_dim(full_base, replica_index * quarter, quarter, 1)
     new_momentum = lax.dynamic_slice_in_dim(full_momentum, replica_index * quarter, quarter, 1)
     return (new_base, new_momentum, keys.astype(jnp.bfloat16), values.astype(jnp.bfloat16))

time: 118 us -> 110 us (0.932)
  the two profiles are of different devices: /device:TPU:1 before, /device:TPU:30 now
where the time goes in v1:
time: 110 us
  waiting for transfers between devices  54.7 us (50%)
  starting transfers between devices  17.2 us (16%)
  local copies, waits for them, and re-layouts  15.2 us (14%)
  matrix products  12.3 us (11%)
  other arithmetic  9.69 us (9%)
    ppermute x4, waiting for transfers between devices, test_the_local_data(): lax.ppermute(met_up, bus_axis, tuple(((b, (b + 1) % vec_out) for b in ran...  27.2 us
    all_to_all x1, waiting for transfers between devices, sent_to_all(): return lax.all_to_all(copies, axis, split_axis=0, concat_axis=0, tiled=True)  24 us
    ppermute x3, starting transfers between devices, test_the_local_data(): lax.ppermute(low, bus_axis, tuple(((b, (b - 1) % vec_out) for b in range(...  10.9 us
    dot_general x1, matrix products, make_adder(): first = jnp.dot(normed, portion[0], preferred_element_type=jnp.float32)  7.63 us
    dynamic_update_slice x4, local copies, waits for them, and re-layouts, test_the_local_data(): lax.dynamic_update_slice_in_dim(back, met_up, (state_now - u) % vec_out *...  5.56 us
    reduce_sum x1, other arithmetic, normalize(): jnp.mean(inputs * inputs, axis=-1, keepdims=True) + epsilon  5.1 us
    dot_general x1, matrix products, make_adder(): second = jnp.dot(normed, portion[1], preferred_element_type=jnp.float32)  4.7 us
    dynamic_update_slice x3, local copies, waits for them, and re-layouts, test_the_local_data(): lax.dynamic_update_slice_in_dim(back, low, (state_now + u) % vec_out * la...  4.7 us
  transfers between devices with their start and end apart: 8, of which 6 were waited for; matrix products, arithmetic and copies ran while one was open for 14% of the time, Pallas kernels for 0%

profile of v1, /device:TPU:30, one launch (start us, length us, event | category | flops | bytes accessed | tf_op | source)
XLA Modules:
  0.0 109.7 jit_solution(16879881470402085400)
XLA Ops:
  0.6 1.5 %fusion.13 = bf16[2,1024,128]{2,1,0:T(8,128)(2,1)S(1)} fusion(f32[2,1024,128]{2,1,0:T(8,128)} %param.7, bf16[1,2,1024,128]{3,2,1,0:T(8,128)(2,1)} %param.9), kind=kLoop, calls=%fused_computation.13 | loop fusion | flops 786432 | bytes 2097152 | tf_op jit(solution)/shard_map/convert_element_type | solution.py:75
  2.1 1.6 %broadcast_in_dim.8 = bf16[4,2,1024,128]{3,2,1,0:T(8,128)(2,1)} broadcast(bf16[2,1024,128]{2,1,0:T(8,128)(2,1)S(1)} %fusion.13), dimensions={1,2,3} | broadcast | bytes 2621440 | tf_op jit(solution)/shard_map/broadcast_in_dim | solution.py:46
  3.7 4.3 %all-to-all-start = ((bf16[4,2,1024,128]{3,2,1,0:T(8,128)(2,1)}), bf16[4,2,1024,128]{3,2,1,0:T(8,128)(2,1)S(1)}, u32[]{:S(2)}, u32[]{:S(2)}) async-start(bf16[4,2,1024,128]{3,2,1,0:T(8,128)(2,1)} %broadcast_in_dim.8), calls=%async_computation | async-start | bytes 4194304 | tf_op jit(solution)/shard_map/all_to_all | solution.py:47
  8.0 24.0 %all-to-all-done = bf16[4,2,1024,128]{3,2,1,0:T(8,128)(2,1)S(1)} async-done(((bf16[4,2,1024,128]{3,2,1,0:T(8,128)(2,1)}), bf16[4,2,1024,128]{3,2,1,0:T(8,128)(2,1)S(1)}, u32[]{:S(2)}, u32[]{:S(2)}) %all-to-all-start) | async-done | bytes 2097184 | tf_op jit(solution)/shard_map/all_to_all | solution.py:47
  32.1 0.3 convert_reduce_fusion
  32.4 2.5 %broadcast_in_dim.9 = bf16[2,8192,128]{2,1,0:T(8,128)(2,1)} broadcast(bf16[]{:T(256)} %constant.73.clone.1), dimensions={} | broadcast | bytes 4194306 | tf_op jit(solution)/shard_map/broadcast_in_dim | solution.py:22
  34.9 2.7 %constant_dynamic-update-slice_fusion.7 = (bf16[2,8192,128]{2,1,0:T(8,128)(2,1)}, bf16[2,1024,128]{2,1,0:T(8,128)(2,1)S(1)}, f32[2,1024,128]{2,1,0:T(8,128)S(1)}) fusion(bf16[2,8192,128]{2,1,0:T(8,128)(2,1)} %broadcast_in_dim.9, s32[]{:T(128)S(6)} %select_n.60, f32[2,1024,128]{2,1,0:T(8,128)} %param.7, f32[2,1024,128]{2,1,0:T(8,128)} %param.8, ...), kind=kLoop, calls=%fused_computation.23 | loop fusion | flops 2097152 | bytes 5242884 | tf_op jit(solution)/shard_map/dynamic_update_slice | solution.py:21
  37.5 1.9 %collective-permute-start = (bf16[2,1024,128]{2,1,0:T(8,128)(2,1)S(1)}, bf16[2,1024,128]{2,1,0:T(8,128)(2,1)}, u32[]{:S(2)}, u32[]{:S(2)}) collective-permute-start(bf16[2,1024,128]{2,1,0:T(8,128)(2,1)S(1)} %get-tuple-element.5), channel_id=1, source_target_pairs={{0,8},{8,16},{16,24},{24,32},{32,40},{40,48},{48,56},{56,0},{1,9},... | collective-permute-start | bytes 1572872 | tf_op jit(solution)/shard_map/ppermute | solution.py:26
  39.5 3.9 %collective-permute-start.1 = (bf16[2,1024,128]{2,1,0:T(8,128)(2,1)S(1)}, bf16[2,1024,128]{2,1,0:T(8,128)(2,1)}, u32[]{:S(2)}, u32[]{:S(2)}) collective-permute-start(bf16[2,1024,128]{2,1,0:T(8,128)(2,1)S(1)} %get-tuple-element.5), channel_id=1, source_target_pairs={{0,56},{8,0},{16,8},{24,16},{32,24},{40,32},{48,40},{56,48},{1,57}... | collective-permute-start | bytes 1572872 | tf_op jit(solution)/shard_map/ppermute | solution.py:33
  43.4 12.1 %collective-permute-done = bf16[2,1024,128]{2,1,0:T(8,128)(2,1)} collective-permute-done((bf16[2,1024,128]{2,1,0:T(8,128)(2,1)S(1)}, bf16[2,1024,128]{2,1,0:T(8,128)(2,1)}, u32[]{:S(2)}, u32[]{:S(2)}) %collective-permute-start) | collective-permute-done | bytes 524320 | tf_op jit(solution)/shard_map/ppermute | solution.py:26
  55.5 0.0 collective-permute-start.2
  55.5 5.1 %fusion = f32[512]{0:T(512)S(1)} fusion(bf16[512,8192]{1,0:T(8,128)(2,1)} %param.5), kind=kLoop, calls=%fused_computation.2 | loop fusion | flops 12582400 | bytes 8390656 | tf_op jit(solution)/shard_map/reduce_sum | solution.py:57
  60.6 0.0 collective-permute-done.1
  60.6 3.3 %collective-permute-start.3 = (bf16[2,1024,128]{2,1,0:T(8,128)(2,1)}, bf16[2,1024,128]{2,1,0:T(8,128)(2,1)}, u32[]{:S(2)}, u32[]{:S(2)}) collective-permute-start(bf16[2,1024,128]{2,1,0:T(8,128)(2,1)} %collective-permute-done.1), channel_id=1, source_target_pairs={{0,56},{8,0},{16,8},{24,16},{32,24},{40,32},{48,40},{56,48},{1,57}... | collective-permute-start | bytes 1572872 | tf_op jit(solution)/shard_map/ppermute | solution.py:33
  63.9 6.3 %collective-permute-done.2 = bf16[2,1024,128]{2,1,0:T(8,128)(2,1)} collective-permute-done((bf16[2,1024,128]{2,1,0:T(8,128)(2,1)}, bf16[2,1024,128]{2,1,0:T(8,128)(2,1)}, u32[]{:S(2)}, u32[]{:S(2)}) %collective-permute-start.2) | collective-permute-done | bytes 524320 | tf_op jit(solution)/shard_map/ppermute | solution.py:26
  70.2 0.1 multiply_add_fusion
  70.3 0.0 copy-start.1
  70.3 0.8 constant_dynamic-slice_fusion
  71.2 3.5 %collective-permute-done.3 = bf16[2,1024,128]{2,1,0:T(8,128)(2,1)} collective-permute-done((bf16[2,1024,128]{2,1,0:T(8,128)(2,1)}, bf16[2,1024,128]{2,1,0:T(8,128)(2,1)}, u32[]{:S(2)}, u32[]{:S(2)}) %collective-permute-start.3) | collective-permute-done | bytes 524320 | tf_op jit(solution)/shard_map/ppermute | solution.py:33
  74.6 3.7 %collective-permute-start.5 = (bf16[2,1024,128]{2,1,0:T(8,128)(2,1)}, bf16[2,1024,128]{2,1,0:T(8,128)(2,1)S(1)}, u32[]{:S(2)}, u32[]{:S(2)}) collective-permute-start(bf16[2,1024,128]{2,1,0:T(8,128)(2,1)} %collective-permute-done.3), channel_id=1, source_target_pairs={{0,56},{8,0},{16,8},{24,16},{32,24},{40,32},{48,40},{56,48},{1,57}... | collective-permute-start | bytes 1572872 | tf_op jit(solution)/shard_map/ppermute | solution.py:33
  78.3 1.9 %constant_dynamic-update-slice_fusion.6 = bf16[2,8192,128]{2,1,0:T(8,128)(2,1)} fusion(bf16[2,8192,128]{2,1,0:T(8,128)(2,1)} %get-tuple-element.4, bf16[2,1024,128]{2,1,0:T(8,128)(2,1)} %collective-permute-done, s32[]{:T(128)S(6)} %select_n.62), kind=kLoop, calls=%fused_computation.22 | loop fusion | bytes 1048580 | tf_op jit(solution)/shard_map/dynamic_update_slice | solution.py:29
  80.2 3.7 %collective-permute-done.4 = bf16[2,1024,128]{2,1,0:T(8,128)(2,1)S(1)} collective-permute-done((bf16[2,1024,128]{2,1,0:T(8,128)(2,1)}, bf16[2,1024,128]{2,1,0:T(8,128)(2,1)S(1)}, u32[]{:S(2)}, u32[]{:S(2)}) %collective-permute-start.4) | collective-permute-done | bytes 524320 | tf_op jit(solution)/shard_map/ppermute | solution.py:26
  83.9 0.0 collective-permute-start.6
  83.9 1.9 %constant_dynamic-update-slice_fusion.5 = bf16[2,8192,128]{2,1,0:T(8,128)(2,1)} fusion(bf16[2,8192,128]{2,1,0:T(8,128)(2,1)} %constant_dynamic-update-slice_fusion.6, bf16[2,1024,128]{2,1,0:T(8,128)(2,1)} %collective-permute-done.1, s32[]{:T(128)S(6)} %select_n.64), kind=kLoop, calls=%fused_computation.21 | loop fusion | bytes 1048580 | tf_op jit(solution)/shard_map/dynamic_update_slice | solution.py:36
  85.8 1.9 %constant_dynamic-update-slice_fusion.4 = bf16[2,8192,128]{2,1,0:T(8,128)(2,1)} fusion(bf16[2,8192,128]{2,1,0:T(8,128)(2,1)} %constant_dynamic-update-slice_fusion.5, bf16[2,1024,128]{2,1,0:T(8,128)(2,1)} %collective-permute-done.2, s32[]{:T(128)S(6)} %select_n.66), kind=kLoop, calls=%fused_computation.20 | loop fusion | bytes 1048580 | tf_op jit(solution)/shard_map/dynamic_update_slice | solution.py:29
  87.8 1.9 %constant_dynamic-update-slice_fusion.3 = bf16[2,8192,128]{2,1,0:T(8,128)(2,1)} fusion(bf16[2,8192,128]{2,1,0:T(8,128)(2,1)} %constant_dynamic-update-slice_fusion.4, bf16[2,1024,128]{2,1,0:T(8,128)(2,1)} %collective-permute-done.3, s32[]{:T(128)S(6)} %select_n.68), kind=kLoop, calls=%fused_computation.19 | loop fusion | bytes 1048580 | tf_op jit(solution)/shard_map/dynamic_update_slice | solution.py:36
  89.7 0.9 constant_dynamic-update-slice_fusion.2
  90.6 0.8 constant_dynamic-update-slice_fusion.1
  91.4 5.1 %collective-permute-done.6 = bf16[2,1024,128]{2,1,0:T(8,128)(2,1)S(1)} collective-permute-done((bf16[2,1024,128]{2,1,0:T(8,128)(2,1)S(1)}, bf16[2,1024,128]{2,1,0:T(8,128)(2,1)S(1)}, u32[]{:S(2)}, u32[]{:S(2)}) %collective-permute-start.6) | collective-permute-done | bytes 524320 | tf_op jit(solution)/shard_map/ppermute | solution.py:26
  96.6 0.8 constant_dynamic-update-slice_fusion
  97.4 7.6 %fusion.7 = bf16[512,128]{1,0:T(8,128)(2,1)} fusion(bf16[2,8192,128]{2,1,0:T(8,128)(2,1)} %constant_dynamic-update-slice_fusion, bf16[512,8192]{1,0:T(8,128)(2,1)} %param.5, f32[8192]{0:T(1024)S(1)} %copy-done.1, f32[512]{0:T(512)S(1)} %add_rsqrt_fusion), kind=kOutput, calls=%fused_computation.10 | convolution fusion | flops 1090584576 | bytes 10651648 | tf_op jit(solution)/shard_map/dot_general | solution.py:68
  105.0 4.7 %fusion.10 = bf16[512,128]{1,0:T(8,128)(2,1)} fusion(bf16[2,8192,128]{2,1,0:T(8,128)(2,1)} %constant_dynamic-update-slice_fusion, bf16[512,8192]{1,0:T(8,128)(2,1)S(1)} %bitcast.14, f32[8192]{0:T(1024)S(1)} %copy-done.1, f32[512]{0:T(512)S(1)} %add_rsqrt_fusion), kind=kOutput, calls=%fused_computation.11 | convolution fusion | flops 1090584576 | bytes 10651648 | tf_op jit(solution)/shard_map/dot_general | solution.py:69
  (11 shorter events, 0.0 us)
Async XLA Ops:
  3.7 28.4 %all-to-all-start = ((bf16[4,2,1024,128]{3,2,1,0:T(8,128)(2,1)}), bf16[4,2,1024,128]{3,2,1,0:T(8,128)(2,1)S(1)}, u32[]{:S(2)}, u32[]{:S(2)}) async-start(bf16[4,2,1024,128]{3,2,1,0:T(8,128)(2,1)} %broadcast_in_dim.8), calls=%async_computation | async-start | bytes 4194304 | tf_op jit(solution)/shard_map/all_to_all | solution.py:47
  37.5 32.6 %copy-start = (f32[2,1024,128]{2,1,0:T(8,128)S(1)}, f32[2,1024,128]{2,1,0:T(8,128)}, u32[]{:S(2)}) copy-start(f32[2,1024,128]{2,1,0:T(8,128)} %param.8) | copy-start | bytes 3145732
  37.5 17.9 %collective-permute-start = (bf16[2,1024,128]{2,1,0:T(8,128)(2,1)S(1)}, bf16[2,1024,128]{2,1,0:T(8,128)(2,1)}, u32[]{:S(2)}, u32[]{:S(2)}) collective-permute-start(bf16[2,1024,128]{2,1,0:T(8,128)(2,1)S(1)} %get-tuple-element.5), channel_id=1, source_target_pairs={{0,8},{8,16},{16,24},{24,32},{32,40},{40,48},{48,56},{56,0},{1,9},... | collective-permute-start | bytes 1572872 | tf_op jit(solution)/shard_map/ppermute | solution.py:26
  39.5 21.1 %collective-permute-start.1 = (bf16[2,1024,128]{2,1,0:T(8,128)(2,1)S(1)}, bf16[2,1024,128]{2,1,0:T(8,128)(2,1)}, u32[]{:S(2)}, u32[]{:S(2)}) collective-permute-start(bf16[2,1024,128]{2,1,0:T(8,128)(2,1)S(1)} %get-tuple-element.5), channel_id=1, source_target_pairs={{0,56},{8,0},{16,8},{24,16},{32,24},{40,32},{48,40},{56,48},{1,57}... | collective-permute-start | bytes 1572872 | tf_op jit(solution)/shard_map/ppermute | solution.py:33
  55.5 14.7 %collective-permute-start.2 = (bf16[2,1024,128]{2,1,0:T(8,128)(2,1)}, bf16[2,1024,128]{2,1,0:T(8,128)(2,1)}, u32[]{:S(2)}, u32[]{:S(2)}) collective-permute-start(bf16[2,1024,128]{2,1,0:T(8,128)(2,1)} %collective-permute-done), channel_id=1, source_target_pairs={{0,8},{8,16},{16,24},{24,32},{32,40},{40,48},{48,56},{56,0},{1,9},... | collective-permute-start | bytes 1572872 | tf_op jit(solution)/shard_map/ppermute | solution.py:26
  60.6 14.0 %collective-permute-start.3 = (bf16[2,1024,128]{2,1,0:T(8,128)(2,1)}, bf16[2,1024,128]{2,1,0:T(8,128)(2,1)}, u32[]{:S(2)}, u32[]{:S(2)}) collective-permute-start(bf16[2,1024,128]{2,1,0:T(8,128)(2,1)} %collective-permute-done.1), channel_id=1, source_target_pairs={{0,56},{8,0},{16,8},{24,16},{32,24},{40,32},{48,40},{56,48},{1,57}... | collective-permute-start | bytes 1572872 | tf_op jit(solution)/shard_map/ppermute | solution.py:33
  70.2 13.7 %collective-permute-start.4 = (bf16[2,1024,128]{2,1,0:T(8,128)(2,1)}, bf16[2,1024,128]{2,1,0:T(8,128)(2,1)S(1)}, u32[]{:S(2)}, u32[]{:S(2)}) collective-permute-start(bf16[2,1024,128]{2,1,0:T(8,128)(2,1)} %collective-permute-done.2), channel_id=1, source_target_pairs={{0,8},{8,16},{16,24},{24,32},{32,40},{40,48},{48,56},{56,0},{1,9},... | collective-permute-start | bytes 1572872 | tf_op jit(solution)/shard_map/ppermute | solution.py:26
  70.3 27.1 %copy-start.1 = (f32[8192]{0:T(1024)S(1)}, f32[8192]{0:T(1024)}, u32[]{:S(2)}) copy-start(f32[8192]{0:T(1024)} %param.6) | copy-start | bytes 98308
  74.6 15.9 %collective-permute-start.5 = (bf16[2,1024,128]{2,1,0:T(8,128)(2,1)}, bf16[2,1024,128]{2,1,0:T(8,128)(2,1)S(1)}, u32[]{:S(2)}, u32[]{:S(2)}) collective-permute-start(bf16[2,1024,128]{2,1,0:T(8,128)(2,1)} %collective-permute-done.3), channel_id=1, source_target_pairs={{0,56},{8,0},{16,8},{24,16},{32,24},{40,32},{48,40},{56,48},{1,57}... | collective-permute-start | bytes 1572872 | tf_op jit(solution)/shard_map/ppermute | solution.py:33
  83.9 12.7 %collective-permute-start.6 = (bf16[2,1024,128]{2,1,0:T(8,128)(2,1)S(1)}, bf16[2,1024,128]{2,1,0:T(8,128)(2,1)S(1)}, u32[]{:S(2)}, u32[]{:S(2)}) collective-permute-start(bf16[2,1024,128]{2,1,0:T(8,128)(2,1)S(1)} %collective-permute-done.4), channel_id=1, source_target_pairs={{0,8},{8,16},{16,24},{24,32},{32,40},{40,48},{48,56},{56,0},{1,9},... | collective-permute-start | bytes 1572872 | tf_op jit(solution)/shard_map/ppermute | solution.py:26
  96.6 8.5 %slice-start = ((s8[8388608]{0:T(1024)(128)(4,1)}), s8[4194304]{0:T(1024)(128)(4,1)S(1)}, s32[]{:S(2)}) async-start(s8[8388608]{0:T(1024)(128)(4,1)} %bitcast.13), calls=%async_computation.1 | async-start | bytes 8388608
  97.4 7.6 %slice-start.1 = ((s8[8388608]{0:T(1024)(128)(4,1)}), s8[4194304]{0:T(1024)(128)(4,1)S(1)}, s32[]{:S(2)}) async-start(s8[8388608]{0:T(1024)(128)(4,1)} %bitcast.13), calls=%async_computation.2 | async-start | bytes 8388608
